TPU v7x, 32 devices: a whole 2x2x4 slice. The times are simulated.
32 devices in a mesh: groups: 2 (over x), weight: 16 (over z, y, core).
Axes of the slice: x: 2, y: 2, z: 4, core: 2. Of those that a mesh axis runs over, the one named last changes fastest.
Arguments:
- hidden: bfloat16 [128, 8192], P(('groups', 'weight')), parts along dimension 0, may hold values from -6 to 6
- norm_gain: float32 [8192], replicated, may hold values from 0.1 to 1.9
- in_weight: bfloat16 [8192, 2, 8192], P(None, None, 'weight'), may hold values from -0.0625 to 0.0625
- conv_weight: float32 [4, 8192], P(None, 'weight'), may hold values from -0.6 to 0.6
- conv_offset: float32 [8192], P('weight'), may hold values from -0.5 to 0.5
- coef_weight: bfloat16 [8192, 544], P('weight'), may hold values from -0.0625 to 0.0625
- step_weight: bfloat16 [512, 8192], P(None, 'weight'), may hold values from -0.25 to 0.25
- step_bias: float32 [8192], P('weight'), may hold values from -3 to 0.5
- log_rates: float32 [16, 8192], P(None, 'weight'), may hold values from 0 to 2.77
- skip_gain: float32 [8192], P('weight'), may hold values from 0.5 to 1.5
- out_weight: bfloat16 [8192, 8192], P('weight'), may hold values from -0.0625 to 0.0625
- ssm_state: bfloat16 [128, 16, 8192], P('groups', None, 'weight'), parts along dimension 0, may hold values from -6 to 6
- conv_state: bfloat16 [128, 3, 8192], P('groups', None, 'weight'), parts along dimension 0, may hold values from -6 to 6
- live_counts: int32 [32], P('groups'), parts along dimension 0, may hold values from 1 to 3, as said below
Outputs:
- mixed: bfloat16 [128, 8192], P(('groups', 'weight')), parts along dimension 0
- new_state: bfloat16 [128, 16, 8192], P('groups', None, 'weight'), parts along dimension 0
- new_conv: bfloat16 [128, 3, 8192], P('groups', None, 'weight'), parts along dimension 0
There are 2 independent parts, one for each index of `groups`. A program takes and returns all parts, laid end to end along the dimension named above; an argument that names none is the same for every part. Nothing has to cross between parts.
Inputs may be any that keep to these rules, and one draw needn't show every extreme that they name: The live rows of a microbatch are its first live_counts rows; the most, 3, is reached by some microbatch.
All inputs are finite; a program needn't handle non-finite values.
Results may differ from a plain program's by a relative error of at most 0.0039.
Values may be sent and summed in bfloat16 or wider, within the bound.
A program may use at most 64 MiB of HBM per device.

v0:
```python
import jax
import jax.numpy as jnp
from jax import lax
from jax.sharding import PartitionSpec as P

NSTATE = 16
DTR = 512
LIVE_MAX = 3


def rms_normed(hidden, norm_gain):
    wide = hidden.astype(jnp.float32)
    factor = lax.rsqrt(jnp.mean(wide * wide, axis=-1, keepdims=True) + 1e-05)
    return (wide * factor * norm_gain).astype(jnp.bfloat16)


def body(
    hidden,
    norm_gain,
    in_weight,
    conv_weight,
    conv_offset,
    coef_weight,
    step_weight,
    step_bias,
    log_rates,
    skip_gain,
    out_weight,
    ssm_state,
    conv_state,
    live_counts,
):
    devices = lax.axis_size("weight")
    rows_dev = hidden.shape[0]
    channels = in_weight.shape[2]
    states_n = ssm_state.shape[1]
    kept = LIVE_MAX
    normed = rms_normed(hidden[:kept], norm_gain)
    joined = in_weight.reshape(in_weight.shape[0], 2 * channels)
    both = jnp.dot(
        lax.all_gather(normed, "weight", axis=0, tiled=True),
        joined,
        preferred_element_type=jnp.float32,
    )
    total_rows = both.shape[0]
    conv_input = both[:, :channels].astype(jnp.bfloat16)
    gate_branch = both[:, channels:]
    state_grid = ssm_state.reshape(devices, rows_dev, states_n, channels)
    conv_grid = conv_state.reshape(devices, rows_dev, 3, channels)
    state_kept = state_grid[:, :kept].reshape(total_rows, states_n, channels)
    conv_kept = conv_grid[:, :kept].reshape(total_rows, 3, channels)
    row_ids = jnp.arange(total_rows, dtype=jnp.int32)
    per_row = jnp.repeat(live_counts, kept, total_repeat_length=total_rows)
    alive = row_ids % kept < per_row
    window = jnp.concatenate([conv_kept, conv_input[:, None, :]], axis=1)
    convolved = jnp.sum(window.astype(jnp.float32) * conv_weight[None], axis=1) + conv_offset
    mixed_x = jax.nn.silu(convolved).astype(jnp.bfloat16)
    partial_low = jnp.dot(mixed_x, coef_weight, preferred_element_type=jnp.float32)
    low_rank = lax.psum(partial_low, "weight")
    step_low = low_rank[:, :DTR].astype(jnp.bfloat16)
    in_coef = low_rank[:, DTR : DTR + NSTATE]
    out_coef = low_rank[:, DTR + NSTATE :]
    step_size = jax.nn.softplus(
        jnp.dot(step_low, step_weight, preferred_element_type=jnp.float32) + step_bias
    )
    x_wide = mixed_x.astype(jnp.float32)
    decays = jnp.exp(-step_size[:, None, :] * jnp.exp(log_rates)[None])
    old_state = state_kept.astype(jnp.float32)
    updated = decays * old_state + step_size[:, None, :] * in_coef[:, :, None] * x_wide[:, None, :]
    readout = jnp.sum(out_coef[:, :, None] * updated, axis=1) + skip_gain * x_wide
    gated_out = jnp.where(alive[:, None], readout * jax.nn.silu(gate_branch), 0.0).astype(
        jnp.bfloat16
    )
    block = lax.slice_in_dim(gated_out, 0, lax.axis_size("weight") * kept, axis=0)
    mixer_term = lax.psum_scatter(
        jnp.dot(block, out_weight, preferred_element_type=jnp.float32),
        "weight",
        scatter_dimension=0,
        tiled=True,
    )
    own_mixed = (hidden[:kept].astype(jnp.float32) + mixer_term).astype(jnp.bfloat16)
    mixed = jnp.concatenate([own_mixed, hidden[kept:]], axis=0)
    state_new_kept = jnp.where(alive[:, None, None], updated, old_state).astype(jnp.bfloat16)
    conv_new_kept = jnp.where(alive[:, None, None], window[:, 1:], conv_kept)
    new_state = jnp.concatenate(
        [state_new_kept.reshape(devices, kept, states_n, channels), state_grid[:, kept:]], axis=1
    ).reshape(ssm_state.shape)
    new_conv = jnp.concatenate(
        [conv_new_kept.reshape(devices, kept, 3, channels), conv_grid[:, kept:]], axis=1
    ).reshape(conv_state.shape)
    return (mixed, new_state, new_conv)


def solution(mesh):
    in_specs = (
        P(("groups", "weight"), None),
        P(),
        P(None, None, "weight"),
        P(None, "weight"),
        P("weight"),
        P("weight", None),
        P(None, "weight"),
        P("weight"),
        P(None, "weight"),
        P("weight"),
        P("weight", None),
        P("groups", None, "weight"),
        P("groups", None, "weight"),
        P("groups"),
    )
    out_specs = (
        P(("groups", "weight"), None),
        P("groups", None, "weight"),
        P("groups", None, "weight"),
    )
    return jax.shard_map(body, mesh=mesh, in_specs=in_specs, out_specs=out_specs, check_vma=False)
```

profile of v0, /device:TPU:0, one launch (start us, length us, event | category | flops | bytes accessed | tf_op | source)
XLA Modules:
  0.0 255.2 jit_solution(7793074444627123706)
XLA Ops:
  7.2 1.1 fusion.4
  8.3 1.0 fusion.8
  9.3 26.3 %all-gather = bf16[16,3,8192]{2,1,0:T(4,128)(2,1)S(1)} all-gather(bf16[1,3,8192]{2,1,0:T(4,128)(2,1)S(1)} %fusion.8), channel_id=1, replica_groups=mesh['groups'=2,'weight'=16] {'weight'}, dimensions={0}, use_global_device_ids=true | all-gather | bytes 835584 | tf_op jit(solution)/shard_map/all_gather | solution.py:41
  35.5 0.7 reshape.164
  36.2 11.4 %copy.19 = bf16[1024,8,2,512]{3,1,2,0:T(8,128)(2,1)S(1)} copy(bf16[1024,8,2,512]{3,2,1,0:T(2,128)(2,1)} %bitcast.24) | data formatting | bytes 33554432
  47.7 3.1 %fusion.26 = f32[48,1024]{1,0:T(8,128)S(1)} fusion(bf16[48,8192]{1,0:T(8,128)(2,1)S(1)} %reshape.164, bf16[8192,1024]{1,0:T(8,128)(2,1)S(1)} %bitcast.23), kind=kOutput, calls=%fused_computation.53 | convolution fusion | flops 805306368 | bytes 17760256 | tf_op jit(solution)/shard_map/dot_general | solution.py:40
  50.9 0.1 reshape.149
  51.1 0.9 fusion.23
  52.3 0.8 gather_fusion
  53.1 0.1 gather.7
  53.1 0.6 fusion.16
  53.8 0.6 fusion.20
  54.3 0.1 copy.18
  54.4 0.6 exp.27
  55.1 81.9 %all-reduce.4.cloned.1.call-done = f32[48,544]{1,0:T(8,128)} async-done(((f32[48,544]{1,0:T(8,128)}), f32[48,544]{1,0:T(8,128)}) %all-reduce.4.cloned.1.call-update) | async-done | bytes 104464 | tf_op jit(solution)/shard_map/psum | solution.py:59
  137.0 0.9 fusion.24
  137.9 0.6 mul.130
  138.5 1.1 fusion.25
  139.8 0.6 mul.121
  140.4 1.7 fusion.1
  142.2 6.2 %fusion.9 = f32[48,8192]{1,0:T(8,128)} fusion(bf16[512,8192]{1,0:T(8,128)(2,1)} %param.26, f32[48,1024]{1,0:T(8,128)S(1)} %fusion.26, f32[48,512]{1,0:T(8,128)S(1)} %reduce_sum.35, f32[512]{0:T(512)} %param.25, pred[48]{0:T(512)(128)(4,1)} %fusion.20, f32[48,512]{1,0:T(8,128)S(1)} %multiply_reduce_fusion.1, f32[512]{0:T(512)} %param.20), kind=kOutput, calls=%fused_computation.31 | convolution fusion | flops 403046400 | bytes 10260528 | tf_op jit(solution)/shard_map/dot_general | solution.py:76
  148.4 0.8 copy-done.3
  149.3 0.1 slice.76
  149.4 0.1 fusion.3
  149.5 0.1 reshape.153
  149.6 0.2 pad_maximum_fusion.2
  149.8 0.7 reshape.154
  150.6 0.6 dynamic-slice.6
  151.8 1.1 pad_maximum_fusion
  152.9 93.7 %all-reduce.6.cloned.1.call-done = f32[48,8192]{1,0:T(8,128)} async-done(((f32[48,8192]{1,0:T(8,128)}), f32[48,8192]{1,0:T(8,128)}) %all-reduce.6.cloned.1.call-update) | async-done | bytes 1572880
  246.6 1.1 fusion.7
  247.7 0.7 pad_maximum_fusion.3
  (45 shorter events, 0.6 us)
Async XLA Ops:
  7.2 43.9 %copy-start = (bf16[512,544]{0,1:T(8,128)(2,1)S(1)}, bf16[512,544]{0,1:T(8,128)(2,1)}, u32[]{:S(2)}) copy-start(bf16[512,544]{0,1:T(8,128)(2,1)} %param.21) | copy-start | bytes 1671172
  7.2 129.8 %all-reduce.4.cloned.1.call-start = ((), (), s32[]{:S(2)}) async-start(), calls=%async_computation | async-start | bytes 245760 | tf_op jit(solution)/shard_map/psum | solution.py:59
  47.6 3.2 %copy-start.7 = (bf16[64,3,512]{2,0,1:T(8,128)(2,1)S(1)}, bf16[64,3,512]{2,0,1:T(8,128)(2,1)}, u32[]{:S(2)}) copy-start(bf16[64,3,512]{2,0,1:T(8,128)(2,1)} %param.28) | copy-start | bytes 589828
  47.6 3.4 %copy-start.10 = (f32[4,512]{1,0:T(4,128)S(1)}, f32[4,512]{1,0:T(4,128)}, u32[]{:S(2)}) copy-start(f32[4,512]{1,0:T(4,128)} %param.19) | copy-start | bytes 24580
  47.7 3.5 %copy-start.8 = (f32[512]{0:T(512)S(1)}, f32[512]{0:T(512)}, u32[]{:S(2)}) copy-start(f32[512]{0:T(512)} %param.20) | copy-start | bytes 6148
  50.8 1.5 copy-start.13
  50.8 1.5 copy-start.1
  50.8 3.6 %copy-start.5 = (bf16[48,1,512]{2,0,1:T(8,128)(2,1)}, bf16[48,1,512]{2,0,1:T(8,128)(2,1)S(1)}, u32[]{:S(2)}) copy-start(bf16[48,1,512]{2,0,1:T(8,128)(2,1)S(1)} %fusion.10) | copy-start | bytes 147460
  50.8 3.6 %copy-start.9 = (f32[16,512]{1,0:T(8,128)S(1)}, f32[16,512]{1,0:T(8,128)}, u32[]{:S(2)}) copy-start(f32[16,512]{1,0:T(8,128)} %param.24) | copy-start | bytes 98308
  50.9 87.6 %copy-start.4 = (bf16[512,512]{1,0:T(8,128)(2,1)S(1)}, bf16[512,512]{1,0:T(8,128)(2,1)}, u32[]{:S(2)}) copy-start(bf16[512,512]{1,0:T(8,128)(2,1)} %param.22) | copy-start | bytes 1572868
  50.9 87.6 %copy-start.12 = (f32[512]{0:T(512)S(1)}, f32[512]{0:T(512)}, u32[]{:S(2)}) copy-start(f32[512]{0:T(512)} %param.23) | copy-start | bytes 6148
  52.1 88.3 %copy-start.2 = (bf16[64,16,512]{2,1,0:T(8,128)(2,1)S(1)}, bf16[64,16,512]{2,1,0:T(8,128)(2,1)}, u32[]{:S(2)}) copy-start(bf16[64,16,512]{2,1,0:T(8,128)(2,1)} %param.27) | copy-start | bytes 3145732
  52.1 194.5 %all-reduce.6.cloned.1.call-start = ((), (), s32[]{:S(2)}) async-start(), calls=%async_computation.1 | async-start | bytes 3145728
  148.4 0.8 copy-start.3
  148.4 1.0 copy-start.6
  148.4 1.0 copy-start.11
  149.2 1.3 copy-start.14
Sparse Core Ops, SparseCore 0:
  52.2 84.7 all-reduce.3
  148.5 98.0 all-reduce.5
where the time goes:
time: 256 us; the launch traced here: 255 us
  waiting for transfers between devices  176 us (69%)
  blocking collectives  26.3 us (10%)
  local copies, waits for them, and re-layouts  18.6 us (7%)
  between operations  15 us (6%)
  matrix products  11.3 us (4%)
  other arithmetic  8.21 us (3%)
    unnamed x3, waiting for transfers between devices  93.8 us
    psum x1, waiting for transfers between devices, body(): low_rank = lax.psum(partial_low, 'weight')  81.9 us
    all_gather x1, blocking collectives, body(): lax.all_gather(normed, 'weight', axis=0, tiled=True)  26.3 us
    unnamed x33, local copies, waits for them, and re-layouts  13.6 us
    dot_general x1, matrix products, body(): jnp.dot(block, out_weight, preferred_element_type=jnp.float32)  6.19 us
  transfers between devices with their start and end apart: 2, of which 2 were waited for; matrix products, arithmetic and copies ran while one was open for 2% of the time, Pallas kernels for 0%

commit v1 on v0

v1 whole, which is shorter than its diff:
```python
import functools

import jax
import jax.numpy as jnp
from jax import lax
from jax.experimental import pallas as pl
from jax.experimental.pallas import tpu as pltpu
from jax.sharding import PartitionSpec as P

NSTATE = 16
DTR = 512
LIVE_MAX = 3
LANES = 128
F32 = jnp.float32
BF16 = jnp.bfloat16
MESH = pl.DeviceIdType.MESH
KSPLIT = 8


def iota(shape, dim):
    return lax.broadcasted_iota(jnp.int32, shape, dim)


def dot(a, b):
    return jnp.dot(a, b, preferred_element_type=F32)


def kernel(
    n, lb,
    hidden, gain, convw, convo, sbias, lograte, skip, live,
    w_hbm, coef_hbm, stepw_hbm, outw_hbm, ssm_hbm, conv_hbm,
    mixed, state_out, conv_out,
    wv, coefv, stepv, outv, ssmv, convv, newconv,
    xs, xg, xf, acc, mx, sgate, lowp, lowr, lowg, inb, outb, step, ro, erate,
    pf, r1, k1, s2, r2, s3, r3, fin,
    wsem, lsem, osem, a_s, a_r, b_s, b_r, c_s, c_r, d_s, d_r, e_s, e_r, f_s, f_r, g_s, g_r, h_s, h_r,
):
    me = lax.axis_index("weight")
    core = me % 2
    y = (me // 2) % 2
    z = me // 4
    outer = n // 4
    depth = hidden.shape[1]
    rows_dev = hidden.shape[0]
    ch = depth // LANES
    blk = LIVE_MAX * ch
    rows = LIVE_MAX * n
    allrows = rows_dev * n
    tiles = wv.shape[0]
    chan = tiles * LANES
    kstep = depth // KSPLIT
    chunks = (DTR + 2 * NSTATE + LANES - 1) // LANES
    wide = DTR + 2 * NSTATE

    def at(zz, yy, cc):
        return zz * 4 + yy * 2 + cc

    def rdma(src, dst, send, recv, dev):
        return pltpu.make_async_remote_copy(
            src_ref=src, dst_ref=dst, send_sem=send, recv_sem=recv,
            device_id={"weight": dev}, device_id_type=MESH,
        )

    wcopies = []
    for s in range(KSPLIT):
        for j in range(tiles):
            cp = pltpu.make_async_copy(
                w_hbm.at[pl.ds(s * kstep, kstep), j], wv.at[j, pl.ds(s * kstep, kstep)], wsem.at[s, j]
            )
            cp.start()
            wcopies.append(cp)
    conv_cp = pltpu.make_async_copy(conv_hbm, convv, lsem.at[0])
    coef_cp = pltpu.make_async_copy(coef_hbm, coefv.at[pl.ds(0, wide)], lsem.at[1])
    step_cp = pltpu.make_async_copy(stepw_hbm, stepv, lsem.at[2])
    ssm_cp = pltpu.make_async_copy(ssm_hbm, ssmv, lsem.at[3])
    out_cp = pltpu.make_async_copy(outw_hbm, outv, lsem.at[4])
    for cp in (conv_cp, coef_cp, step_cp, ssm_cp, out_cp):
        cp.start()

    barrier = pltpu.get_barrier_semaphore()
    for k in range(1, n):
        pl.semaphore_signal(barrier, inc=1, device_id={"weight": (me + k) % n}, device_id_type=MESH)

    h = hidden[...].astype(F32)
    factor = lax.rsqrt(jnp.mean(h * h, axis=-1, keepdims=True) + 1e-05)
    nm = h * factor * gain[...]
    for c in range(ch):
        xs[pl.ds(c, rows_dev, stride=ch), :] = nm[:, c * LANES : (c + 1) * LANES]
    xg[me] = xs[pl.ds(0, blk), :].astype(BF16)
    coefv[pl.ds(wide, chunks * LANES - wide), :] = jnp.zeros((chunks * LANES - wide, chan), BF16)
    pl.semaphore_wait(barrier, n - 1)

    def widen(b):
        xf[pl.ds(pl.multiple_of(b * blk, 8), blk), :] = xg[b].astype(F32)

    sends = []
    for k in range(1, outer):
        cp = rdma(xg.at[me], xg.at[me], a_s.at[k], a_r.at[k], at((z + k) % outer, y, core))
        cp.start()
        sends.append(cp)
    ypeer = at(z, 1 - y, core)
    cpeer = at(z, y, 1 - core)
    for k in range(outer):
        zz = (z + outer - k) % outer
        b = at(zz, y, core)
        if k:
            rdma(xg.at[b], xg.at[b], a_s.at[k], a_r.at[k], ypeer).wait_recv()
        cp = rdma(xg.at[b], xg.at[b], b_s.at[k], b_r.at[k], ypeer)
        cp.start()
        sends.append(cp)
        cp = rdma(xg.at[b], xg.at[b], c_s.at[k], c_r.at[k], cpeer)
        cp.start()
        sends.append(cp)
        widen(b)
    for k in range(outer):
        b = at((z + outer - k) % outer, 1 - y, core)
        rdma(xg.at[b], xg.at[b], b_s.at[k], b_r.at[k], ypeer).wait_recv()
        cp = rdma(xg.at[b], xg.at[b], c_s.at[outer + k], c_r.at[outer + k], cpeer)
        cp.start()
        sends.append(cp)
        widen(b)
    for k in range(2 * outer):
        zz = (z + 2 * outer - k) % outer
        b = at(zz, y if k < outer else 1 - y, 1 - core)
        rdma(xg.at[b], xg.at[b], c_s.at[k], c_r.at[k], cpeer).wait_recv()
        widen(b)

    lane = iota((LANES, 4 * LANES), 1)
    spread = jnp.where(
        (lane % (2 * LANES) == 2 * iota((LANES, 4 * LANES), 0) + lane // (2 * LANES)), 1.0, 0.0
    ).astype(BF16)
    acc[...] = jnp.zeros_like(acc)
    for cp in wcopies:
        cp.wait()
    per = kstep // LANES

    @pl.loop(0, KSPLIT)
    def _(s):
        tops, lows = [], []
        for i in range(per):
            xc = xf[pl.ds(s * per + i, rows, stride=ch), :].astype(BF16)
            e = dot(xc, spread).astype(BF16)
            tops.append(e[:, : 2 * LANES])
            lows.append(e[:, 2 * LANES :])
        lhs = jnp.concatenate(
            [jnp.concatenate(tops, axis=1), jnp.concatenate(lows, axis=1)], axis=0
        )
        rhs = jnp.concatenate(
            [
                wv.at[j].reshape(2 * depth, LANES)[pl.ds(pl.multiple_of(s * 2 * kstep, 16), 2 * kstep), :]
                for j in range(tiles)
            ],
            axis=1,
        )
        acc[...] += dot(lhs, rhs)

    conv_cp.wait()
    ci = acc[pl.ds(0, rows), :].astype(BF16)
    cif = ci.astype(F32)
    r_at, c_at = iota((rows, allrows), 0), iota((rows, allrows), 1)
    pick = jnp.where(
        (c_at % rows_dev < LIVE_MAX) & (c_at // rows_dev * LIVE_MAX + c_at % rows_dev == r_at), 1.0, 0.0
    ).astype(BF16)
    total = cif * convw[pl.ds(3, 1), :] + convo[...]
    for t in range(3):
        total = total + dot(pick, convv[t]) * convw[pl.ds(t, 1), :]
    x = (total / (1.0 + jnp.exp(-total))).astype(BF16)
    mx[...] = x.astype(F32)

    coef_cp.wait()
    part = lax.dot_general(x, coefv[...], (((1,), (1,)), ((), ())), preferred_element_type=F32)
    for c in range(chunks):
        lowp[pl.ds(c * rows, rows), :] = part[:, c * LANES : (c + 1) * LANES]
    if n * lb > chunks * rows:
        lowp[pl.ds(chunks * rows, n * lb - chunks * rows), :] = jnp.zeros(
            (n * lb - chunks * rows, LANES), F32
        )

    def low_at(ref, d):
        return ref.at[pl.ds(pl.multiple_of(d * lb, 8), lb)]

    for k in range(1, n):
        d = (me + k) % n
        cp = rdma(low_at(lowp, d), lowr.at[k], d_s.at[k], d_r.at[k], d)
        cp.start()
        sends.append(cp)

    g = acc[pl.ds(rows, rows), :]
    sgate[...] = g / (1.0 + jnp.exp(-g))
    erate[...] = jnp.exp(lograte[...])
    row4 = iota((allrows, chan), 0)
    count4 = jnp.zeros((allrows, chan), jnp.int32)
    for m in range(n):
        count4 = jnp.where(row4 // rows_dev == m, live[m], count4)
    alive4 = row4 % rows_dev < count4
    t_at, s_at = iota((allrows, rows), 1), iota((allrows, rows), 0)
    put = jnp.where(
        (s_at % rows_dev < LIVE_MAX) & (s_at // rows_dev * LIVE_MAX + s_at % rows_dev == t_at), 1.0, 0.0
    ).astype(BF16)
    for t in range(3):
        new = convv[t + 1].astype(F32) if t < 2 else dot(put, ci)
        newconv[t] = jnp.where(alive4, new, convv[t].astype(F32)).astype(BF16)
    conv_done = pltpu.make_async_copy(newconv, conv_out, osem.at[0])
    conv_done.start()

    own = low_at(lowp, me)[...]
    for k in range(1, n):
        rdma(lowr.at[k], lowr.at[k], d_s.at[k], d_r.at[k], ypeer).wait_recv()
        own = own + lowr[k]
    low_at(lowg, me)[...] = own
    for k in range(1, n):
        d = (me + k) % n
        cp = rdma(low_at(lowg, me), low_at(lowg, me), e_s.at[k], e_r.at[k], d)
        cp.start()
        sends.append(cp)
    for k in range(1, n):
        src = low_at(lowg, (me + n - k) % n)
        rdma(src, src, e_s.at[k], e_r.at[k], ypeer).wait_recv()

    step_cp.wait()
    low = jnp.concatenate(
        [lowg[pl.ds(c * rows, rows), :] for c in range(DTR // LANES)], axis=1
    ).astype(BF16)
    v = dot(low, stepv[...]) + sbias[...]
    step[...] = jnp.maximum(v, 0.0) + jnp.log1p(jnp.exp(-jnp.abs(v)))
    coefs = lowg[pl.ds(DTR // LANES * rows, rows), :]
    for q in range(NSTATE):
        inb[pl.ds(q, rows, stride=NSTATE), :] = jnp.broadcast_to(coefs[:, q : q + 1], (rows, LANES))
        outb[pl.ds(q, rows, stride=NSTATE), :] = jnp.broadcast_to(
            coefs[:, NSTATE + q : NSTATE + q + 1], (rows, LANES)
        )
    ssm_cp.wait()

    @pl.loop(0, n)
    def _(m):
        count = live[m]
        for j in range(LIVE_MAX):
            r = m * LIVE_MAX + j
            old = ssmv[m * rows_dev + j].astype(F32)
            st = step[pl.ds(r, 1), :]
            xr = mx[pl.ds(r, 1), :]
            at_r = pl.ds(pl.multiple_of(r * NSTATE, NSTATE), NSTATE)
            inc = jnp.concatenate([inb[at_r, :]] * tiles, axis=1)
            outc = jnp.concatenate([outb[at_r, :]] * tiles, axis=1)
            upd = jnp.exp(-st * erate[...]) * old + st * inc * xr
            ro[pl.ds(r, 1), :] = jnp.sum(outc * upd, axis=0, keepdims=True)
            keep = jnp.full(old.shape, count, jnp.int32) > j
            ssmv[m * rows_dev + j] = jnp.where(keep, upd, old).astype(BF16)

    state_done = pltpu.make_async_copy(ssmv, state_out, osem.at[1])
    state_done.start()

    row3 = iota((rows, chan), 0)
    count3 = jnp.zeros((rows, chan), jnp.int32)
    for m in range(n):
        count3 = jnp.where(row3 // LIVE_MAX == m, live[m], count3)
    read = (ro[...] + skip[...] * mx[...]) * sgate[...]
    gated = jnp.where(row3 % LIVE_MAX < count3, read, 0.0).astype(BF16)

    out_cp.wait()
    ntile = 8

    @pl.loop(0, ch // ntile)
    def _(t):
        p = dot(gated, outv[:, pl.ds(pl.multiple_of(t * ntile * LANES, LANES), ntile * LANES)])
        for i in range(ntile):
            pf[pl.ds(t * ntile + i, rows, stride=ch), :] = p[:, i * LANES : (i + 1) * LANES]

    def pf_at(d):
        return pf.at[pl.ds(pl.multiple_of(d * blk, 8), blk)]

    order = [(k, yy) for yy in (0, 1) for k in range(outer)]
    for i, (k, flip) in enumerate(order):
        zz = (z + k) % outer
        yy = 1 - y if flip == 0 else y
        cp = rdma(pf_at(at(zz, yy, 1 - core)), r1.at[i], f_s.at[i], f_r.at[i], cpeer)
        cp.start()
        sends.append(cp)
    for i, (k, flip) in enumerate(order):
        zz = (z + k) % outer
        yy = 1 - y if flip == 0 else y
        rdma(r1.at[i], r1.at[i], f_s.at[i], f_r.at[i], cpeer).wait_recv()
        both = pf_at(at(zz, yy, core))[...] + r1[i]
        if flip == 0:
            s2[k] = both.astype(BF16)
            cp = rdma(s2.at[k], r2.at[k], g_s.at[k], g_r.at[k], ypeer)
            cp.start()
            sends.append(cp)
        else:
            k1[k] = both
    for k in list(range(1, outer)) + [0]:
        rdma(r2.at[k], r2.at[k], g_s.at[k], g_r.at[k], ypeer).wait_recv()
        both = k1[k] + r2[k].astype(F32)
        if k:
            s3[k] = both.astype(BF16)
            cp = rdma(s3.at[k], r3.at[k], h_s.at[k], h_r.at[k], at((z + k) % outer, y, core))
            cp.start()
            sends.append(cp)
    for k in range(1, outer):
        rdma(r3.at[k], r3.at[k], h_s.at[k], h_r.at[k], ypeer).wait_recv()
        both = both + r3[k].astype(F32)
    fin[pl.ds(0, blk), :] = both
    fin[pl.ds(blk, ch * rows_dev - blk), :] = jnp.zeros((ch * rows_dev - blk, LANES), F32)
    for c in range(ch):
        cols = slice(c * LANES, (c + 1) * LANES)
        mixed[:, cols] = (hidden[:, cols].astype(F32) + fin[pl.ds(c, rows_dev, stride=ch), :]).astype(BF16)
    for cp in sends:
        cp.wait_send()
    conv_done.wait()
    state_done.wait()


def body(
    hidden, norm_gain, in_weight, conv_weight, conv_offset, coef_weight, step_weight,
    step_bias, log_rates, skip_gain, out_weight, ssm_state, conv_state, live_counts,
):
    n = lax.axis_size("weight")
    rows_dev, depth = hidden.shape
    chan = in_weight.shape[2]
    tiles = chan // LANES
    ch = depth // LANES
    rows = LIVE_MAX * n
    allrows = rows_dev * n
    blk = LIVE_MAX * ch
    outer = n // 4
    chunks = (DTR + 2 * NSTATE + LANES - 1) // LANES
    lb = -(-(chunks * rows) // (8 * n)) * 8
    weight = in_weight.reshape(depth, 2, tiles, LANES).transpose(0, 2, 1, 3)
    vmem = pl.BlockSpec(memory_space=pltpu.VMEM)
    smem = pl.BlockSpec(memory_space=pltpu.SMEM)
    hbm = pl.BlockSpec(memory_space=pl.ANY)
    dma = pltpu.SemaphoreType.DMA
    V = pltpu.VMEM
    mixed, new_state, new_conv = pl.pallas_call(
        functools.partial(kernel, n, lb),
        out_shape=(
            jax.ShapeDtypeStruct(hidden.shape, BF16),
            jax.ShapeDtypeStruct(ssm_state.shape, BF16),
            jax.ShapeDtypeStruct((3, allrows, chan), BF16),
        ),
        in_specs=[vmem] * 7 + [smem] + [hbm] * 6,
        out_specs=(vmem, hbm, hbm),
        scratch_shapes=[
            V((tiles, depth, 2, LANES), BF16),
            V((chunks * LANES, chan), BF16),
            V(step_weight.shape, BF16),
            V(out_weight.shape, BF16),
            V(ssm_state.shape, BF16),
            V((3, allrows, chan), BF16),
            V((3, allrows, chan), BF16),
            V((rows_dev * ch, LANES), F32),
            V((n, blk, LANES), BF16),
            V((n * blk, LANES), F32),
            V((2 * rows, chan), F32),
            V((rows, chan), F32),
            V((rows, chan), F32),
            V((n * lb, LANES), F32),
            V((n, lb, LANES), F32),
            V((n * lb, LANES), F32),
            V((rows * NSTATE, LANES), F32),
            V((rows * NSTATE, LANES), F32),
            V((rows, chan), F32),
            V((rows, chan), F32),
            V((NSTATE, chan), F32),
            V((n * blk, LANES), F32),
            V((2 * outer, blk, LANES), F32),
            V((outer, blk, LANES), F32),
            V((outer, blk, LANES), BF16),
            V((outer, blk, LANES), BF16),
            V((outer, blk, LANES), BF16),
            V((outer, blk, LANES), BF16),
            V((rows_dev * ch, LANES), F32),
            dma((KSPLIT, tiles)),
            dma((5,)),
            dma((2,)),
            dma((outer,)), dma((outer,)),
            dma((outer,)), dma((outer,)),
            dma((2 * outer,)), dma((2 * outer,)),
            dma((n,)), dma((n,)),
            dma((n,)), dma((n,)),
            dma((2 * outer,)), dma((2 * outer,)),
            dma((outer,)), dma((outer,)),
            dma((outer,)), dma((outer,)),
        ],
        compiler_params=pltpu.CompilerParams(
            collective_id=0, has_side_effects=True, vmem_limit_bytes=58 * 1024 * 1024
        ),
        name="mixer",
    )(
        hidden, norm_gain[None], conv_weight, conv_offset[None], step_bias[None], log_rates,
        skip_gain[None], live_counts,
        weight, coef_weight.T, step_weight, out_weight, ssm_state, conv_state.transpose(1, 0, 2),
    )
    return mixed, new_state, new_conv.transpose(1, 0, 2)


def solution(mesh):
    in_specs = (
        P(("groups", "weight"), None),
        P(),
        P(None, None, "weight"),
        P(None, "weight"),
        P("weight"),
        P("weight", None),
        P(None, "weight"),
        P("weight"),
        P(None, "weight"),
        P("weight"),
        P("weight", None),
        P("groups", None, "weight"),
        P("groups", None, "weight"),
        P("groups"),
    )
    out_specs = (
        P(("groups", "weight"), None),
        P("groups", None, "weight"),
        P("groups", None, "weight"),
    )
    return jax.shard_map(body, mesh=mesh, in_specs=in_specs, out_specs=out_specs, check_vma=False)
```

time: 256 us -> 62.9 us (0.25)
  waiting for transfers between devices: 176 us -> 0 us
  Pallas kernels: 0 us -> 56.6 us
  blocking collectives: 26.3 us -> 0 us
  between operations: 15 us -> 0.65 us
  local copies, waits for them, and re-layouts: 18.6 us -> 5.37 us
  matrix products: 11.3 us -> 0 us
  other arithmetic: 8.21 us -> 0 us
    unnamed x3 -> x0, waiting for transfers between devices: 93.8 us -> none
    psum x1 -> x0, waiting for transfers between devices: 81.9 us -> none  [body(): low_rank = lax.psum(partial_low, 'weight')]
    pallas_call x0 -> x1, Pallas kernels: none -> 56.6 us  [body(): pl.pallas_call(functools.partial(kernel, n, lb), out_shape=(jax.ShapeDtyp...]
    all_gather x1 -> x0, blocking collectives: 26.3 us -> none  [body(): lax.all_gather(normed, 'weight', axis=0, tiled=True)]
    dot_general x4 -> x0, matrix products: 11.3 us -> none  [the longest x1 6.19 us: body(): jnp.dot(block, out_weight, preferred_element_type=jnp.float32)]
    unnamed x33 -> x3, local copies, waits for them, and re-layouts: 13.6 us -> 5.37 us
    convert_element_type x3 -> x0, other arithmetic: 2.86 us -> none  [the longest x1 1.71 us: body(): jnp.where(alive[:, None, None], updated, old_state).astype(jnp.bfloat16)]
  transfers between devices with their start and end apart: 2 -> 0, of which waited for: 2 -> 0; matrix products, arithmetic and copies ran while one was open for 2% -> 0% of each run, Pallas kernels for 0% -> 0%
where the time goes in v1:
time: 62.9 us; the launch traced here: 62.6 us
  Pallas kernels  56.6 us (90%)
  local copies, waits for them, and re-layouts  5.37 us (9%)
  between operations  0.65 us (1%)
    pallas_call x1, Pallas kernels, body(): pl.pallas_call(functools.partial(kernel, n, lb), out_shape=(jax.ShapeDtyp...  56.6 us
    unnamed x3, local copies, waits for them, and re-layouts  5.37 us

profile of v1, /device:TPU:0, one launch (start us, length us, event | category | flops | bytes accessed | tf_op | source)
XLA Modules:
  0.0 62.6 jit_solution(871025944891938559)
XLA Ops:
  0.6 56.6 %mixer.1 = (bf16[4,8192]{1,0:T(4,128)(2,1)}, bf16[64,16,512]{2,1,0:T(8,128)(2,1)}, bf16[3,64,512]{2,1,0:T(8,128)(2,1)}) custom-call(bf16[4,8192]{1,0:T(4,128)(2,1)} %hidden.1, f32[1,8192]{1,0:T(1,128)} %bitcast.14, f32[4,512]{1,0:T(4,128)} %convw.1, f32[1,512]{1,0:T(1,128)} %bitcast.15, f32[1,512]{1,0:T(1,128)} %bitcast.16, f32[16,512]{1,0:T(8,128)} %lograte.1, ...), custom_call_target="tpu_custom_call" | custom-call | tf_op jit(solution)/shard_map/mixer/pallas_call | solution.py:334
  57.3 1.5 %copy.20 = bf16[4,8192]{1,0:T(4,128)(2,1)} copy(bf16[4,8192]{1,0:T(4,128)(2,1)} %get-tuple-element.12) | data formatting | bytes 131072
  58.8 2.3 %copy.21 = bf16[64,16,512]{2,1,0:T(8,128)(2,1)} copy(bf16[64,16,512]{2,1,0:T(8,128)(2,1)} %get-tuple-element.13) | data formatting | bytes 2097152
  61.0 1.6 %copy.22 = bf16[64,3,512]{2,0,1:T(8,128)(2,1)} copy(bf16[64,3,512]{2,0,1:T(8,128)(2,1)} %bitcast.13) | data formatting | bytes 393216

commit v2 on v1

--- a/solution.py
+++ b/solution.py
@@ -15,6 +15,7 @@
 BF16 = jnp.bfloat16
 MESH = pl.DeviceIdType.MESH
 KSPLIT = 8
+PARTS = 4
 
 
 def iota(shape, dim):
@@ -49,6 +50,9 @@
     tiles = wv.shape[0]
     chan = tiles * LANES
     kstep = depth // KSPLIT
+    chq = ch // PARTS
+    bq = LIVE_MAX * chq
+    span = n * bq
     chunks = (DTR + 2 * NSTATE + LANES - 1) // LANES
     wide = DTR + 2 * NSTATE
 
@@ -86,73 +90,103 @@
     nm = h * factor * gain[...]
     for c in range(ch):
         xs[pl.ds(c, rows_dev, stride=ch), :] = nm[:, c * LANES : (c + 1) * LANES]
-    xg[me] = xs[pl.ds(0, blk), :].astype(BF16)
+    for q in range(PARTS):
+        for j in range(LIVE_MAX):
+            xg[q, me, pl.ds(j * chq, chq), :] = xs[pl.ds(j * ch + q * chq, chq), :].astype(BF16)
     coefv[pl.ds(wide, chunks * LANES - wide), :] = jnp.zeros((chunks * LANES - wide, chan), BF16)
     pl.semaphore_wait(barrier, n - 1)
 
-    def widen(b):
-        xf[pl.ds(pl.multiple_of(b * blk, 8), blk), :] = xg[b].astype(F32)
-
     sends = []
-    for k in range(1, outer):
-        cp = rdma(xg.at[me], xg.at[me], a_s.at[k], a_r.at[k], at((z + k) % outer, y, core))
+    ypeer = at(z, 1 - y, core)
+    cpeer = at(z, y, 1 - core)
+
+    def near(k):
+        low, high = z, outer - 1 - z
+        least = jnp.minimum(low, high)
+        both = (k + 1) // 2 * (1 if k % 2 else -1)
+        one = (k - least) * jnp.where(high > low, 1, -1)
+        return z + jnp.where(k <= 2 * least, both, one)
+
+    places = [z] + [near(k) for k in range(1, outer)]
+
+    def move(q, b, send, recv, slot, dev):
+        return rdma(xg.at[q, b], xg.at[q, b], send.at[q, slot], recv.at[q, slot], dev)
+
+    def go(cp):
         cp.start()
         sends.append(cp)
-    ypeer = at(z, 1 - y, core)
-    cpeer = at(z, y, 1 - core)
-    for k in range(outer):
-        zz = (z + outer - k) % outer
-        b = at(zz, y, core)
-        if k:
-            rdma(xg.at[b], xg.at[b], a_s.at[k], a_r.at[k], ypeer).wait_recv()
-        cp = rdma(xg.at[b], xg.at[b], b_s.at[k], b_r.at[k], ypeer)
-        cp.start()
-        sends.append(cp)
-        cp = rdma(xg.at[b], xg.at[b], c_s.at[k], c_r.at[k], cpeer)
-        cp.start()
-        sends.append(cp)
-        widen(b)
-    for k in range(outer):
-        b = at((z + outer - k) % outer, 1 - y, core)
-        rdma(xg.at[b], xg.at[b], b_s.at[k], b_r.at[k], ypeer).wait_recv()
-        cp = rdma(xg.at[b], xg.at[b], c_s.at[outer + k], c_r.at[outer + k], cpeer)
-        cp.start()
-        sends.append(cp)
-        widen(b)
-    for k in range(2 * outer):
-        zz = (z + 2 * outer - k) % outer
-        b = at(zz, y if k < outer else 1 - y, 1 - core)
-        rdma(xg.at[b], xg.at[b], c_s.at[k], c_r.at[k], cpeer).wait_recv()
-        widen(b)
+
+    for q in range(PARTS):
+        for k in range(outer - 1, 0, -1):
+            cp = rdma(xg.at[q, me], xg.at[q, me], a_s.at[q, k], a_r.at[q, z], at(places[k], y, core))
+            go(cp)
+        go(move(q, me, b_s, b_r, z, ypeer))
+        go(move(q, me, c_s, c_r, 2 * z + y, cpeer))
+
+    def forward_z(q):
+        for k in range(1, outer):
+            p = places[k]
+            b = at(p, y, core)
+            rdma(xg.at[q, b], xg.at[q, b], a_s.at[q, k], a_r.at[q, p], ypeer).wait_recv()
+            go(move(q, b, b_s, b_r, p, ypeer))
+            go(move(q, b, c_s, c_r, 2 * p + y, cpeer))
+
+    def forward_y(q):
+        for p in places:
+            b = at(p, 1 - y, core)
+            move(q, b, b_s, b_r, p, ypeer).wait_recv()
+            go(move(q, b, c_s, c_r, 2 * p + 1 - y, cpeer))
+
+    def arrived(q):
+        for p in places:
+            for yy in (y, 1 - y):
+                move(q, at(p, yy, 1 - core), c_s, c_r, 2 * p + yy, cpeer).wait_recv()
+        xf[pl.ds(q * span, span), :] = jnp.concatenate([xg[q, b] for b in range(n)], axis=0).astype(F32)
 
     lane = iota((LANES, 4 * LANES), 1)
     spread = jnp.where(
         (lane % (2 * LANES) == 2 * iota((LANES, 4 * LANES), 0) + lane // (2 * LANES)), 1.0, 0.0
     ).astype(BF16)
-    acc[...] = jnp.zeros_like(acc)
-    for cp in wcopies:
-        cp.wait()
     per = kstep // LANES
 
-    @pl.loop(0, KSPLIT)
-    def _(s):
-        tops, lows = [], []
-        for i in range(per):
-            xc = xf[pl.ds(s * per + i, rows, stride=ch), :].astype(BF16)
-            e = dot(xc, spread).astype(BF16)
-            tops.append(e[:, : 2 * LANES])
-            lows.append(e[:, 2 * LANES :])
+    def project(s):
+        first = s * per
+        q, base = first // chq, first % chq
+        x = jnp.concatenate(
+            [xf[pl.ds(q * span + base + i, rows, stride=chq), :] for i in range(per)], axis=0
+        ).astype(BF16)
+        e = dot(x, spread).astype(BF16)
         lhs = jnp.concatenate(
-            [jnp.concatenate(tops, axis=1), jnp.concatenate(lows, axis=1)], axis=0
+            [
+                jnp.concatenate(
+                    [e[i * rows : (i + 1) * rows, h * 2 * LANES : (h + 1) * 2 * LANES] for i in range(per)],
+                    axis=1,
+                )
+                for h in range(2)
+            ],
+            axis=0,
         )
+        for j in range(tiles):
+            wcopies[s * tiles + j].wait()
         rhs = jnp.concatenate(
-            [
-                wv.at[j].reshape(2 * depth, LANES)[pl.ds(pl.multiple_of(s * 2 * kstep, 16), 2 * kstep), :]
-                for j in range(tiles)
-            ],
+            [wv.at[j].reshape(2 * depth, LANES)[pl.ds(s * 2 * kstep, 2 * kstep), :] for j in range(tiles)],
             axis=1,
         )
-        acc[...] += dot(lhs, rhs)
+        if s == 0:
+            acc[...] = dot(lhs, rhs)
+        else:
+            acc[...] += dot(lhs, rhs)
+
+    forward_z(0)
+    forward_y(0)
+    for q in range(PARTS):
+        if q + 1 < PARTS:
+            forward_z(q + 1)
+        arrived(q)
+        for s in range(q * KSPLIT // PARTS, (q + 1) * KSPLIT // PARTS):
+            project(s)
+            if q + 1 < PARTS and s == q * KSPLIT // PARTS:
+                forward_y(q + 1)
 
     conv_cp.wait()
     ci = acc[pl.ds(0, rows), :].astype(BF16)
@@ -258,48 +292,56 @@
     gated = jnp.where(row3 % LIVE_MAX < count3, read, 0.0).astype(BF16)
 
     out_cp.wait()
-    ntile = 8
-
-    @pl.loop(0, ch // ntile)
-    def _(t):
-        p = dot(gated, outv[:, pl.ds(pl.multiple_of(t * ntile * LANES, LANES), ntile * LANES)])
-        for i in range(ntile):
-            pf[pl.ds(t * ntile + i, rows, stride=ch), :] = p[:, i * LANES : (i + 1) * LANES]
-
-    def pf_at(d):
-        return pf.at[pl.ds(pl.multiple_of(d * blk, 8), blk)]
-
-    order = [(k, yy) for yy in (0, 1) for k in range(outer)]
-    for i, (k, flip) in enumerate(order):
-        zz = (z + k) % outer
-        yy = 1 - y if flip == 0 else y
-        cp = rdma(pf_at(at(zz, yy, 1 - core)), r1.at[i], f_s.at[i], f_r.at[i], cpeer)
-        cp.start()
-        sends.append(cp)
-    for i, (k, flip) in enumerate(order):
-        zz = (z + k) % outer
-        yy = 1 - y if flip == 0 else y
-        rdma(r1.at[i], r1.at[i], f_s.at[i], f_r.at[i], cpeer).wait_recv()
-        both = pf_at(at(zz, yy, core))[...] + r1[i]
-        if flip == 0:
-            s2[k] = both.astype(BF16)
-            cp = rdma(s2.at[k], r2.at[k], g_s.at[k], g_r.at[k], ypeer)
-            cp.start()
-            sends.append(cp)
-        else:
-            k1[k] = both
-    for k in list(range(1, outer)) + [0]:
-        rdma(r2.at[k], r2.at[k], g_s.at[k], g_r.at[k], ypeer).wait_recv()
-        both = k1[k] + r2[k].astype(F32)
-        if k:
-            s3[k] = both.astype(BF16)
-            cp = rdma(s3.at[k], r3.at[k], h_s.at[k], h_r.at[k], at((z + k) % outer, y, core))
-            cp.start()
-            sends.append(cp)
-    for k in range(1, outer):
-        rdma(r3.at[k], r3.at[k], h_s.at[k], h_r.at[k], ypeer).wait_recv()
-        both = both + r3[k].astype(F32)
-    fin[pl.ds(0, blk), :] = both
+    cols = chq * LANES
+
+    def pf_at(h, d):
+        return pf.at[pl.ds(pl.multiple_of(h * span + d * bq, 8), bq)]
+
+    def stage1(h):
+        p = dot(gated, outv[:, pl.ds(h * cols, cols)])
+        for i in range(chq):
+            pf[pl.ds(h * span + i, rows, stride=chq), :] = p[:, i * LANES : (i + 1) * LANES]
+        for yy in (1 - y, y):
+            for k in range(outer - 1, -1, -1):
+                slot = 2 * places[k] + yy
+                go(rdma(pf_at(h, at(places[k], yy, 1 - core)), r1.at[h, slot], f_s.at[h, slot], f_r.at[h, slot], cpeer))
+
+    def paired(h, k, yy):
+        slot = 2 * places[k] + yy
+        rdma(r1.at[h, slot], r1.at[h, slot], f_s.at[h, slot], f_r.at[h, slot], cpeer).wait_recv()
+        return pf_at(h, at(places[k], yy, core))[...] + r1[h, slot]
+
+    def stage2(h):
+        for k in range(outer - 1, -1, -1):
+            p = places[k]
+            s2[h, p] = paired(h, k, 1 - y).astype(BF16)
+            go(rdma(s2.at[h, p], r2.at[h, p], g_s.at[h, p], g_r.at[h, p], ypeer))
+
+    def stage3(h):
+        for k in range(outer - 1, -1, -1):
+            p = places[k]
+            both = paired(h, k, y)
+            rdma(r2.at[h, p], r2.at[h, p], g_s.at[h, p], g_r.at[h, p], ypeer).wait_recv()
+            both = both + r2[h, p].astype(F32)
+            if k:
+                s3[h, p] = both.astype(BF16)
+                go(rdma(s3.at[h, p], r3.at[h, z], h_s.at[h, p], h_r.at[h, z], at(p, y, core)))
+            else:
+                k1[h] = both
+
+    def stage4(h):
+        both = k1[h]
+        for k in range(1, outer):
+            p = places[k]
+            rdma(r3.at[h, p], r3.at[h, p], h_s.at[h, p], h_r.at[h, p], ypeer).wait_recv()
+            both = both + r3[h, p].astype(F32)
+        for j in range(LIVE_MAX):
+            fin[pl.ds(j * ch + h * chq, chq), :] = both[j * chq : (j + 1) * chq]
+
+    for t in range(PARTS + 3):
+        for late, stage in enumerate((stage1, stage2, stage3, stage4)):
+            if 0 <= t - late < PARTS:
+                stage(t - late)
     fin[pl.ds(blk, ch * rows_dev - blk), :] = jnp.zeros((ch * rows_dev - blk, LANES), F32)
     for c in range(ch):
         cols = slice(c * LANES, (c + 1) * LANES)
@@ -308,6 +350,25 @@
         cp.wait_send()
     conv_done.wait()
     state_done.wait()
+
+
+def hand_out(mixed, state, conv, mixed_out, state_out, conv_out, mixed_v, state_v, conv_v, sem_in, sem_out):
+    half = state.shape[0] // 2
+    trips = [
+        (state.at[pl.ds(0, half)], state_v.at[pl.ds(0, half)], state_out.at[pl.ds(0, half)]),
+        (state.at[pl.ds(half, half)], state_v.at[pl.ds(half, half)], state_out.at[pl.ds(half, half)]),
+        (conv, conv_v, conv_out),
+        (mixed, mixed_v, mixed_out),
+    ]
+    ins = [pltpu.make_async_copy(a, v, sem_in.at[i]) for i, (a, v, _) in enumerate(trips)]
+    outs = [pltpu.make_async_copy(v, o, sem_out.at[i]) for i, (_, v, o) in enumerate(trips)]
+    for cp in ins:
+        cp.start()
+    for first, second in zip(ins, outs):
+        first.wait()
+        second.start()
+    for cp in outs:
+        cp.wait()
 
 
 def body(
@@ -323,6 +384,7 @@
     allrows = rows_dev * n
     blk = LIVE_MAX * ch
     outer = n // 4
+    bq = blk // PARTS
     chunks = (DTR + 2 * NSTATE + LANES - 1) // LANES
     lb = -(-(chunks * rows) // (8 * n)) * 8
     weight = in_weight.reshape(depth, 2, tiles, LANES).transpose(0, 2, 1, 3)
@@ -349,7 +411,7 @@
             V((3, allrows, chan), BF16),
             V((3, allrows, chan), BF16),
             V((rows_dev * ch, LANES), F32),
-            V((n, blk, LANES), BF16),
+            V((PARTS, n, bq, LANES), BF16),
             V((n * blk, LANES), F32),
             V((2 * rows, chan), F32),
             V((rows, chan), F32),
@@ -363,24 +425,24 @@
             V((rows, chan), F32),
             V((NSTATE, chan), F32),
             V((n * blk, LANES), F32),
-            V((2 * outer, blk, LANES), F32),
-            V((outer, blk, LANES), F32),
-            V((outer, blk, LANES), BF16),
-            V((outer, blk, LANES), BF16),
-            V((outer, blk, LANES), BF16),
-            V((outer, blk, LANES), BF16),
+            V((PARTS, 2 * outer, bq, LANES), F32),
+            V((PARTS, bq, LANES), F32),
+            V((PARTS, outer, bq, LANES), BF16),
+            V((PARTS, outer, bq, LANES), BF16),
+            V((PARTS, outer, bq, LANES), BF16),
+            V((PARTS, outer, bq, LANES), BF16),
             V((rows_dev * ch, LANES), F32),
             dma((KSPLIT, tiles)),
             dma((5,)),
             dma((2,)),
-            dma((outer,)), dma((outer,)),
-            dma((outer,)), dma((outer,)),
-            dma((2 * outer,)), dma((2 * outer,)),
+            dma((PARTS, outer)), dma((PARTS, outer)),
+            dma((PARTS, outer)), dma((PARTS, outer)),
+            dma((PARTS, 2 * outer)), dma((PARTS, 2 * outer)),
             dma((n,)), dma((n,)),
             dma((n,)), dma((n,)),
-            dma((2 * outer,)), dma((2 * outer,)),
-            dma((outer,)), dma((outer,)),
-            dma((outer,)), dma((outer,)),
+            dma((PARTS, 2 * outer)), dma((PARTS, 2 * outer)),
+            dma((PARTS, outer)), dma((PARTS, outer)),
+            dma((PARTS, outer)), dma((PARTS, outer)),
         ],
         compiler_params=pltpu.CompilerParams(
             collective_id=0, has_side_effects=True, vmem_limit_bytes=58 * 1024 * 1024
@@ -391,6 +453,14 @@
         skip_gain[None], live_counts,
         weight, coef_weight.T, step_weight, out_weight, ssm_state, conv_state.transpose(1, 0, 2),
     )
+    mixed, new_state, new_conv = pl.pallas_call(
+        hand_out,
+        out_shape=tuple(jax.ShapeDtypeStruct(a.shape, a.dtype) for a in (mixed, new_state, new_conv)),
+        in_specs=[hbm] * 3,
+        out_specs=(hbm,) * 3,
+        scratch_shapes=[V(a.shape, a.dtype) for a in (mixed, new_state, new_conv)] + [dma((4,)), dma((4,))],
+        name="hand_out",
+    )(mixed, new_state, new_conv)
     return mixed, new_state, new_conv.transpose(1, 0, 2)
 
 

time: 62.9 us -> 62.2 us (0.989)
  local copies, waits for them, and re-layouts: 5.37 us -> 0 us
  Pallas kernels: 56.6 us -> 61.2 us
    unnamed x3 -> x0, local copies, waits for them, and re-layouts: 5.37 us -> none
    pallas_call x1, Pallas kernels: 56.6 us -> 59.1 us  [body(): pl.pallas_call(functools.partial(kernel, n, lb), out_shape=(jax.ShapeDtyp...]
    pallas_call x0 -> x1, Pallas kernels: none -> 2.15 us  [body(): pl.pallas_call(hand_out, out_shape=tuple((jax.ShapeDtypeStruct(a.shape, a...]
where the time goes in v2:
time: 62.2 us; the launch traced here: 62 us
  Pallas kernels  61.2 us (98%)
  between operations  0.8 us (1%)
    pallas_call x1, Pallas kernels, body(): pl.pallas_call(functools.partial(kernel, n, lb), out_shape=(jax.ShapeDtyp...  59.1 us
    pallas_call x1, Pallas kernels, body(): pl.pallas_call(hand_out, out_shape=tuple((jax.ShapeDtypeStruct(a.shape, a...  2.15 us

profile of v2, /device:TPU:0, one launch (start us, length us, event | category | flops | bytes accessed | tf_op | source)
XLA Modules:
  0.0 62.0 jit_solution(5956282042883455415)
XLA Ops:
  0.6 59.1 %mixer.1 = (bf16[4,8192]{1,0:T(4,128)(2,1)}, bf16[64,16,512]{2,1,0:T(8,128)(2,1)}, bf16[3,64,512]{2,1,0:T(8,128)(2,1)}) custom-call(bf16[4,8192]{1,0:T(4,128)(2,1)} %hidden.1, f32[1,8192]{1,0:T(1,128)} %bitcast.13, f32[4,512]{1,0:T(4,128)} %convw.1, f32[1,512]{1,0:T(1,128)} %bitcast.14, f32[1,512]{1,0:T(1,128)} %bitcast.15, f32[16,512]{1,0:T(8,128)} %lograte.1, ...), custom_call_target="tpu_custom_call" | custom-call | tf_op jit(solution)/shard_map/mixer/pallas_call | solution.py:396
  59.7 2.2 %hand_out.1 = (bf16[4,8192]{1,0:T(4,128)(2,1)}, bf16[64,16,512]{2,1,0:T(8,128)(2,1)}, bf16[3,64,512]{2,1,0:T(8,128)(2,1)}) custom-call(bf16[4,8192]{1,0:T(4,128)(2,1)} %get-tuple-element.9.mixed, bf16[64,16,512]{2,1,0:T(8,128)(2,1)} %get-tuple-element.10.state, bf16[3,64,512]{2,1,0:T(8,128)(2,1)} %get-tuple-element.11.conv), custom_call_target="tpu_custom_call" | custom-call | tf_op jit(solution)/shard_map/hand_out/pallas_call | solution.py:456
